TPU v7x, 32 devices: a whole 2x2x4 slice. The times are simulated.
32 devices in a mesh: comp: 2 (over y), tile: 4 (over x, core), lev: 4 (over z).
Axes of the slice: x: 2, y: 2, z: 4, core: 2. Of those that a mesh axis runs over, the one named last changes fastest.
Arguments:
- thermal_anomaly: float32 [2, 80, 2048], P('comp', 'lev', 'tile'), may hold values from -6 to 6
- right_face_transport_ratio: float32 [2, 80, 2048], P('comp', 'lev', 'tile'), may hold values from -0.45 to 0.45
- species_ratios: float32 [2, 40, 80, 2048], P('comp', None, 'lev', 'tile'), may hold values from 0.1 to 3
- lateral_spreading_number: float32 [2, 80, 2048], P('comp', 'lev', 'tile'), may hold values from 0.05 to 0.2
- depth_physics_operator: float32 [2, 80, 80], P('comp'), may hold values from -1 to 1, as said below
- exchange_weight_table: float32 [2048, 4], P('tile'), may hold values from 0.05 to 0.5
- sky_point_of_entry: int32 [2048, 4], P('tile'), may hold values from 0 to 2047, as said below
- water_indicator: int32 [2048], P('tile'), may hold values 0 or 1
Outputs:
- thermal_anomaly_ending: float32 [2, 80, 2048], P('comp', 'lev', 'tile')
- species_ratios_ending: float32 [2, 40, 80, 2048], P('comp', None, 'lev', 'tile')
Inputs may be any that keep to these rules, and one draw needn't show every extreme that they name: The ocean cells of each block of 512 (cells b * 512 to (b + 1) * 512 - 1) take their sources near the matching cells of one atmosphere block p(b), p a permutation of the blocks: sky_point_of_entry[j, k] lies cyclically within 128 cells of p(b) * 512 + (j mod 512). `depth_physics_operator`: each matrix has diagonal entries between 0.5 and 1.
All inputs are finite; a program needn't handle non-finite values. No bound on the sum of `water_indicator` on one device may be relied on, other than what follows from the above.
Results may differ from a plain program's by a relative error of at most 0.0003.
Values sent between devices are 32-bit elements; how exact they have to be, the bound alone decides.
No kernel may reach another device: no remote copies, remote signals or barrier semaphores. Data moves between devices by JAX's collectives and lax.ppermute only.
A program may use at most 64 MiB of HBM per device.

v0:
```python
import jax
import jax.numpy as jnp
from jax import lax
from jax.sharding import PartitionSpec as P

NFLUX = 4


def extended(x, sides, width):
    for axis, dim in sides:
        devices, length = (lax.axis_size(axis), x.shape[dim])
        up = [(i, (i + 1) % devices) for i in range(devices)]
        down = [(j, i) for i, j in up]
        last = lax.slice_in_dim(x, length - width, length, axis=dim)
        first = lax.slice_in_dim(x, 0, width, axis=dim)
        before = lax.ppermute(last, axis, up)
        after = lax.ppermute(first, axis, down)
        x = jnp.concatenate([before, x, after], axis=dim)
    return x


def passed_along(value, axis, steps):
    count = lax.axis_size(axis)
    first, last = (max(0, -steps), min(count, count - steps))
    return lax.ppermute(value, axis, [(source, source + steps) for source in range(first, last)])


def advance(padded, lateral_spreading_number):
    middle = padded[..., 1:-1]
    before = padded[..., :-2]
    after = padded[..., 2:]
    speed = middle[:, 1:2]
    speed_left = before[:, 1:2]
    flux_right = jnp.maximum(speed, 0.0) * middle + jnp.minimum(speed, 0.0) * after
    flux_left = jnp.maximum(speed_left, 0.0) * before + jnp.minimum(speed_left, 0.0) * middle
    tendency = -(flux_right - flux_left)
    thermal_energy = middle[:, 0]
    heat_next = thermal_energy + (
        tendency[:, 0]
        + lateral_spreading_number * (before[:, 0] - 2.0 * thermal_energy + after[:, 0])
    )
    tracer_next = middle[:, 2:] + tendency[:, 2:]
    return jnp.concatenate([heat_next[:, None], speed, tracer_next], axis=1)


def body(
    thermal_anomaly,
    right_face_transport_ratio,
    species_ratios,
    lateral_spreading_number,
    depth_physics_operator,
    exchange_weight_table,
    sky_point_of_entry,
    water_indicator,
):
    sections = lax.axis_size("comp")
    is_ocean = lax.axis_index("comp") >= sections // 2
    joined_quantities = jnp.concatenate(
        [thermal_anomaly[:, None], right_face_transport_ratio[:, None], species_ratios], axis=1
    )
    for substep in range(2):
        padded = extended(joined_quantities, (("tile", 3),), 1)
        advanced = advance(padded, lateral_spreading_number)
        if substep == 0:
            joined_quantities = advanced
        else:
            joined_quantities = jnp.where(is_ocean, joined_quantities, advanced)
    column = joined_quantities[0, 0]
    level_count = column.shape[0]
    offset = lax.axis_index("lev") * level_count
    matrix = depth_physics_operator[0]
    my_rows = lax.dynamic_slice_in_dim(matrix, offset, level_count, 0)
    blended_profiles = jnp.dot(
        my_rows,
        lax.all_gather(column, "lev", axis=0, tiled=True),
        precision=lax.Precision.HIGHEST,
        preferred_element_type=jnp.float32,
    )
    surface = jnp.concatenate(
        [blended_profiles[0:1], joined_quantities[0, 2 : 2 + NFLUX - 1, 0]], 0
    )
    whole = lax.all_gather(surface, "tile", axis=1, tiled=True)
    received = passed_along(whole, "comp", sections // 2)
    picked = received[:, sky_point_of_entry]
    remapped = jnp.sum(picked * exchange_weight_table, -1)
    updated = surface + 0.5 * (remapped - surface)
    at_sea = jnp.logical_and(
        jnp.logical_and(is_ocean, lax.axis_index("lev") == 0), water_indicator == 1
    )
    renewed_interface_values = jnp.where(at_sea[None, :], updated, surface)
    thermal_anomaly_ending = blended_profiles.at[0].set(renewed_interface_values[0])[None]
    species_ratios_ending = (
        joined_quantities[:, 2:].at[0, 0 : NFLUX - 1, 0].set(renewed_interface_values[1:])
    )
    return (thermal_anomaly_ending, species_ratios_ending)


def solution(mesh):
    in_specs = (
        P("comp", "lev", "tile"),
        P("comp", "lev", "tile"),
        P("comp", None, "lev", "tile"),
        P("comp", "lev", "tile"),
        P("comp", None, None),
        P("tile", None),
        P("tile", None),
        P("tile"),
    )
    out_specs = (P("comp", "lev", "tile"), P("comp", None, "lev", "tile"))
    return jax.shard_map(body, mesh=mesh, in_specs=in_specs, out_specs=out_specs, check_vma=False)
```

profile of v0, /device:TPU:0, one launch (start us, length us, event | category | flops | bytes accessed | tf_op | source)
XLA Modules:
  0.0 121.7 jit_solution(12595853146820664689)
XLA Ops:
  0.7 3.1 %copy.245 = f32[1,40,20,512]{3,0,2,1:T(1,128)S(1)} copy(f32[1,40,20,512]{3,1,2,0:T(8,128)} %param.14) | data formatting | bytes 3276800 | tf_op args[2]
  3.8 2.4 %fusion.8 = f32[1,42,20,512]{3,0,2,1:T(1,128)S(1)} fusion(f32[1,1,20,512]{3,0,2,1:T(1,128)S(1)} %bitcast.89, f32[1,40,20,512]{3,0,2,1:T(1,128)S(1)} %copy.245, f32[1,1,20,512]{3,0,2,1:T(1,128)S(1)} %bitcast.100), kind=kLoop, calls=%fused_computation.17 | loop fusion | flops 860160 | bytes 3440640 | tf_op jit(solution)/shard_map/concatenate | solution.py:58
  6.2 2.1 %fusion.40 = (f32[1,42,20,1]{3,0,2,1:T(1,128)}, f32[1,42,20,1]{3,0,2,1:T(1,128)}) fusion(f32[1,42,20,512]{3,0,2,1:T(1,128)S(1)} %fusion.8), kind=kLoop, calls=%fused_computation.80 | loop fusion | bytes 13440 | tf_op jit(solution)/shard_map/slice | solution.py:15
  8.3 2.4 %collective-permute-start = (f32[1,42,20,1]{3,0,2,1:T(1,128)}, f32[1,42,20,1]{3,0,2,1:T(1,128)S(1)}, u32[]{:S(2)}, u32[]{:S(2)}) collective-permute-start(f32[1,42,20,1]{3,0,2,1:T(1,128)} %get-tuple-element.56), channel_id=1, source_target_pairs={{4,0},{8,4},{12,8},{0,12},{5,1},{9,5},{13,9},{1,13},{6,2},{10,6},{... | collective-permute-start | bytes 10088 | tf_op jit(solution)/shard_map/ppermute | solution.py:17
  10.8 0.6 copy_bitcast_fusion
  11.8 9.5 %collective-permute-done = f32[1,42,20,1]{3,0,2,1:T(1,128)S(1)} collective-permute-done((f32[1,42,20,1]{3,0,2,1:T(1,128)}, f32[1,42,20,1]{3,0,2,1:T(1,128)S(1)}, u32[]{:S(2)}, u32[]{:S(2)}) %collective-permute-start) | collective-permute-done | bytes 3392 | tf_op jit(solution)/shard_map/ppermute | solution.py:17
  21.3 0.9 collective-permute-done.1
  22.3 12.0 %fusion.5 = (f32[1,42,20,513]{3,0,2,1:T(1,128)S(1)}, f32[1,42,20,513]{3,0,2,1:T(1,128)S(1)}) fusion(f32[1,1,20,512]{3,0,2,1:T(1,128)S(1)} %bitcast.90, f32[1,42,20,1]{3,0,2,1:T(1,128)S(1)} %collective-permute-done, f32[1,40,20,512]{3,0,2,1:T(1,128)S(1)} %copy.245, f32[1,1,20,512]{3,0,2,1:T(1,128)S(1)} %bitcast.101, ...), kind=kLoop, calls=%fused_computation.10 | loop fusion | flops 2585520 | bytes 5174400 | tf_op jit(solution)/shard_map/concatenate | solution.py:18
  34.4 4.9 %fusion.17 = f32[1,42,20,512]{3,0,2,1:T(1,128)S(1)} fusion(f32[1,42,20,513]{3,0,2,1:T(1,128)S(1)} %get-tuple-element.55, f32[1,42,20,513]{3,0,2,1:T(1,128)S(1)} %get-tuple-element.54, f32[20,512]{1,0:T(8,128)S(1)} %get-tuple-element.63, f32[20,512]{1,0:T(8,128)S(1)} %get-tuple-element.62, f32[20,512]{1,0:T(8,128)S(1)} %copy-done.5, ...), kind=kLoop, calls=%fused_computation.30 | loop fusion | flops 4300800 | bytes 7045120 | tf_op jit(solution)/shard_map/neg | solution.py:36
  39.3 2.2 %slice_add_fusion.1 = f32[1,40,20,512]{3,0,2,1:T(1,128)S(1)} fusion(f32[1,42,20,512]{3,0,2,1:T(1,128)S(1)} %fusion.17, f32[1,40,20,512]{3,1,2,0:T(8,128)S(1)} %copy-done.2), kind=kLoop, calls=%fused_computation.33 | loop fusion | flops 409600 | bytes 4915200 | tf_op jit(solution)/shard_map/add | solution.py:42
  41.8 2.4 %fusion.9 = f32[1,42,20,512]{3,0,2,1:T(1,128)S(1)} fusion(f32[1,1,20,512]{3,0,2,1:T(1,128)S(1)} %bitcast.92, f32[1,40,20,512]{3,0,2,1:T(1,128)S(1)} %slice_add_fusion.1, f32[1,1,20,512]{3,0,2,1:T(1,128)S(1)} %bitcast.97), kind=kLoop, calls=%fused_computation.18 | loop fusion | flops 860160 | bytes 3440640 | tf_op jit(solution)/shard_map/concatenate | solution.py:43
  44.2 2.1 %fusion.39 = (f32[1,42,20,1]{3,0,2,1:T(1,128)}, f32[1,42,20,1]{3,0,2,1:T(1,128)}) fusion(f32[1,42,20,512]{3,0,2,1:T(1,128)S(1)} %fusion.9), kind=kLoop, calls=%fused_computation.79 | loop fusion | bytes 13440 | tf_op jit(solution)/shard_map/slice | solution.py:15
  46.2 1.2 collective-permute-start.2
  47.4 10.3 %collective-permute-done.2 = f32[1,42,20,1]{3,0,2,1:T(1,128)} collective-permute-done((f32[1,42,20,1]{3,0,2,1:T(1,128)}, f32[1,42,20,1]{3,0,2,1:T(1,128)}, u32[]{:S(2)}, u32[]{:S(2)}) %collective-permute-start.2) | collective-permute-done | bytes 3392 | tf_op jit(solution)/shard_map/ppermute | solution.py:17
  57.7 1.0 collective-permute-done.3
  58.7 13.0 %fusion.7 = (f32[1,42,20,513]{3,0,2,1:T(1,128)S(1)}, f32[1,42,20,513]{3,0,2,1:T(1,128)S(1)}) fusion(f32[1,1,20,512]{3,0,2,1:T(1,128)S(1)} %bitcast.93, f32[1,42,20,1]{3,0,2,1:T(1,128)} %collective-permute-done.2, f32[1,40,20,512]{3,0,2,1:T(1,128)S(1)} %slice_add_fusion.1, f32[1,1,20,512]{3,0,2,1:T(1,128)S(1)} %bitcast.98, ...), kind=kLoop, calls=%fused_computation.12 | loop fusion | flops 2585520 | bytes 5174400 | tf_op jit(solution)/shard_map/concatenate | solution.py:18
  71.9 4.9 %fusion.18 = f32[1,42,20,512]{3,0,2,1:T(1,128)S(1)} fusion(f32[1,42,20,513]{3,0,2,1:T(1,128)S(1)} %get-tuple-element.51, f32[1,42,20,513]{3,0,2,1:T(1,128)S(1)} %get-tuple-element.50, f32[20,512]{1,0:T(8,128)S(1)} %get-tuple-element.59, f32[20,512]{1,0:T(8,128)S(1)} %get-tuple-element.58, f32[20,512]{1,0:T(8,128)S(1)} %copy-done.6, ...), kind=kLoop, calls=%fused_computation.31 | loop fusion | flops 4300800 | bytes 7045120 | tf_op jit(solution)/shard_map/neg | solution.py:36
  76.8 0.2 add_bitcast_fusion
  77.0 3.3 %slice_add_fusion = f32[1,40,20,512]{3,0,2,1:T(1,128)S(1)} fusion(f32[1,40,20,512]{3,0,2,1:T(1,128)S(1)} %slice_add_fusion.1, f32[1,42,20,512]{3,0,2,1:T(1,128)S(1)} %fusion.18), kind=kLoop, calls=%fused_computation.32 | loop fusion | flops 409600 | bytes 4915200 | tf_op jit(solution)/shard_map/add | solution.py:42
  80.3 2.4 %fusion.10 = f32[1,42,20,512]{3,0,2,1:T(1,128)S(1)} fusion(f32[1,1,20,512]{3,0,2,1:T(1,128)S(1)} %bitcast.95, f32[1,40,20,512]{3,0,2,1:T(1,128)S(1)} %slice_add_fusion, f32[1,1,20,512]{3,0,2,1:T(1,128)S(1)} %add_bitcast_fusion), kind=kLoop, calls=%fused_computation.19 | loop fusion | flops 860160 | bytes 3440640 | tf_op jit(solution)/shard_map/concatenate | solution.py:43
  82.7 1.0 copy_select_fusion
  83.8 1.2 %copy-done.1 = f32[1,42,20,512]{3,1,0,2:T(8,128)} copy-done((f32[1,42,20,512]{3,1,0,2:T(8,128)}, f32[1,42,20,512]{3,1,0,2:T(8,128)S(1)}, u32[]{:S(2)}) %copy-start.1) | copy-done | bytes 1720344
  85.0 13.7 %all-gather = f32[1,1,80,512]{3,1,0,2:T(1,128)S(1)} all-gather(f32[1,1,20,512]{3,1,0,2:T(1,128)S(1)} %slice.171), channel_id=2, replica_groups=mesh['comp'=2,'tile'=4,'lev'=4] {'lev'}, dimensions={2}, use_global_device_ids=true | all-gather | bytes 204800 | tf_op jit(solution)/shard_map/all_gather | solution.py:75
  98.8 0.2 fusion.19
  99.0 5.2 %all_gather.7 = f32[4,2048]{1,0:T(4,128)S(1)} all-gather(f32[4,512]{1,0:T(4,128)S(1)} %pad_maximum_fusion.7), channel_id=1, replica_groups=mesh['comp'=2,'tile'=4,'lev'=4] {'tile'}, dimensions={1}, use_global_device_ids=true | all-gather | bytes 40960 | tf_op jit(solution)/shard_map/all_gather | solution.py:82
  104.2 3.4 %collective-permute-start.4 = (f32[4,2048]{1,0:T(4,128)S(1)}, f32[4,2048]{1,0:T(4,128)S(1)}, u32[]{:S(2)}, u32[]{:S(2)}) collective-permute-start(f32[4,2048]{1,0:T(4,128)S(1)} %all_gather.7), channel_id=1, source_target_pairs={{0,16},{1,17},{2,18},{3,19},{4,20},{5,21},{6,22},{7,23},{8,24},{9,... | collective-permute-start | bytes 98312 | tf_op jit(solution)/shard_map/ppermute | solution.py:25
  107.8 3.0 %slice.175 = f32[1,40,20,512]{3,1,0,2:T(8,128)} slice(f32[1,42,20,512]{3,1,0,2:T(8,128)} %copy-done.1), slice={[0:1], [2:42], [0:20], [0:512]} | slice | bytes 3276800 | tf_op jit(solution)/shard_map/slice | solution.py:93
  110.8 0.4 copy.252
  111.2 5.5 %gather_fusion = f32[2048,4]{1,0:T(8,128)S(1)} fusion(f32[4,2048]{0,1:T(8,128)S(1)} %copy.252, s32[2048]{0:T(1024)S(1)} %broadcast_clamp_fusion), kind=kCustom, calls=%fused_computation | custom fusion | bytes 73728 | tf_op jit(solution)/shard_map/gather | solution.py:84
  116.7 2.8 %multiply_reduce_fusion = f32[512,4]{1,0:T(8,128)S(1)} fusion(f32[512,4,4]{2,1,0:T(4,128)S(1)} %bitcast.88, f32[512,4]{1,0:T(8,128)S(1)} %copy.253), kind=kLoop, calls=%fused_computation.34 | loop fusion | flops 14336 | bytes 49152 | tf_op jit(solution)/shard_map/reduce_sum | solution.py:85
  119.7 0.7 copy.256
  120.4 1.4 %scatter.9 = f32[1,40,20,512]{3,1,0,2:T(8,128)} dynamic-update-slice(f32[1,40,20,512]{3,1,0,2:T(8,128)} %slice.175, f32[1,3,1,512]{3,1,0,2:T(4,128)S(1)} %slice_bitcast_fusion.6, s32[]{:T(128)} %constant.77.clone.1, s32[]{:T(128)} %constant.77.clone.1, s32[]{:T(128)} %constant.77.clone.1, s32[]{:T(128)} %constant.77.clone.1) | dynamic-update-slice | bytes 12292 | tf_op jit(solution)/shard_map/scatter | solution.py:93
  (51 shorter events, 1.1 us)
Async XLA Ops:
  0.6 98.1 %copy-start = (f32[1,80,80]{2,1,0:T(8,128)S(1)}, f32[1,80,80]{2,1,0:T(8,128)}, u32[]{:S(2)}) copy-start(f32[1,80,80]{2,1,0:T(8,128)} %param.16) | copy-start | bytes 76804
  0.6 3.2 %copy-start.3 = (f32[1,20,512]{2,0,1:T(1,128)S(1)}, f32[1,20,512]{2,0,1:T(1,128)}, u32[]{:S(2)}) copy-start(f32[1,20,512]{2,0,1:T(1,128)} %param.13) | copy-start | bytes 122884
  0.7 3.2 %copy-start.4 = (f32[1,20,512]{2,0,1:T(1,128)S(1)}, f32[1,20,512]{2,0,1:T(1,128)}, u32[]{:S(2)}) copy-start(f32[1,20,512]{2,0,1:T(1,128)} %param.12) | copy-start | bytes 122884
  6.2 5.2 %copy-start.12 = (s32[512,4]{0,1:T(4,128)S(1)}, s32[512,4]{0,1:T(4,128)}, u32[]{:S(2)}) copy-start(s32[512,4]{0,1:T(4,128)} %param.18) | copy-start | bytes 24580
  8.3 13.0 %collective-permute-start = (f32[1,42,20,1]{3,0,2,1:T(1,128)}, f32[1,42,20,1]{3,0,2,1:T(1,128)S(1)}, u32[]{:S(2)}, u32[]{:S(2)}) collective-permute-start(f32[1,42,20,1]{3,0,2,1:T(1,128)} %get-tuple-element.56), channel_id=1, source_target_pairs={{4,0},{8,4},{12,8},{0,12},{5,1},{9,5},{13,9},{1,13},{6,2},{10,6},{... | collective-permute-start | bytes 10088 | tf_op jit(solution)/shard_map/ppermute | solution.py:17
  10.7 11.5 %collective-permute-start.1 = (f32[1,42,20,1]{3,0,2,1:T(1,128)}, f32[1,42,20,1]{3,0,2,1:T(1,128)S(1)}, u32[]{:S(2)}, u32[]{:S(2)}) collective-permute-start(f32[1,42,20,1]{3,0,2,1:T(1,128)} %get-tuple-element.57), channel_id=1, source_target_pairs={{0,4},{4,8},{8,12},{12,0},{1,5},{5,9},{9,13},{13,1},{2,6},{6,10},{... | collective-permute-start | bytes 10088 | tf_op jit(solution)/shard_map/ppermute | solution.py:16
  11.8 22.6 %copy-start.5 = (f32[20,512]{1,0:T(8,128)S(1)}, f32[20,512]{1,0:T(8,128)}, u32[]{:S(2)}) copy-start(f32[20,512]{1,0:T(8,128)} %get-tuple-element.64) | copy-start | bytes 122884
  11.8 22.6 %copy-start.7 = (f32[20,512]{1,0:T(8,128)S(1)}, f32[20,512]{1,0:T(8,128)}, u32[]{:S(2)}) copy-start(f32[20,512]{1,0:T(8,128)} %get-tuple-element.65) | copy-start | bytes 122884
  34.4 4.9 %copy-start.2 = (f32[1,40,20,512]{3,1,2,0:T(8,128)S(1)}, f32[1,40,20,512]{3,1,2,0:T(8,128)}, u32[]{:S(2)}) copy-start(f32[1,40,20,512]{3,1,2,0:T(8,128)} %param.14) | copy-start | bytes 4915204
  39.3 2.3 %copy-start.9 = (f32[1,20,512]{2,0,1:T(1,128)S(1)}, f32[1,20,512]{2,0,1:T(1,128)}, u32[]{:S(2)}) copy-start(f32[1,20,512]{2,0,1:T(1,128)} %param.15) | copy-start | bytes 122884
  46.2 11.5 %collective-permute-start.2 = (f32[1,42,20,1]{3,0,2,1:T(1,128)}, f32[1,42,20,1]{3,0,2,1:T(1,128)}, u32[]{:S(2)}, u32[]{:S(2)}) collective-permute-start(f32[1,42,20,1]{3,0,2,1:T(1,128)} %get-tuple-element.52), channel_id=1, source_target_pairs={{4,0},{8,4},{12,8},{0,12},{5,1},{9,5},{13,9},{1,13},{6,2},{10,6},{... | collective-permute-start | bytes 10088 | tf_op jit(solution)/shard_map/ppermute | solution.py:17
  47.4 11.3 %collective-permute-start.3 = (f32[1,42,20,1]{3,0,2,1:T(1,128)}, f32[1,42,20,1]{3,0,2,1:T(1,128)}, u32[]{:S(2)}, u32[]{:S(2)}) collective-permute-start(f32[1,42,20,1]{3,0,2,1:T(1,128)} %get-tuple-element.53), channel_id=1, source_target_pairs={{0,4},{4,8},{8,12},{12,0},{1,5},{5,9},{9,13},{13,1},{2,6},{6,10},{... | collective-permute-start | bytes 10088 | tf_op jit(solution)/shard_map/ppermute | solution.py:16
  47.4 24.4 %copy-start.6 = (f32[20,512]{1,0:T(8,128)S(1)}, f32[20,512]{1,0:T(8,128)}, u32[]{:S(2)}) copy-start(f32[20,512]{1,0:T(8,128)} %get-tuple-element.64) | copy-start | bytes 122884
  47.4 24.4 %copy-start.8 = (f32[20,512]{1,0:T(8,128)S(1)}, f32[20,512]{1,0:T(8,128)}, u32[]{:S(2)}) copy-start(f32[20,512]{1,0:T(8,128)} %get-tuple-element.65) | copy-start | bytes 122884
  71.8 4.9 %copy-start.10 = (f32[1,20,512]{2,0,1:T(1,128)S(1)}, f32[1,20,512]{2,0,1:T(1,128)}, u32[]{:S(2)}) copy-start(f32[1,20,512]{2,0,1:T(1,128)} %param.15) | copy-start | bytes 122884
  82.7 24.9 %copy-start.13 = (s32[512]{0:T(512)S(1)}, s32[512]{0:T(512)}, u32[]{:S(2)}) copy-start(s32[512]{0:T(512)} %param.19) | copy-start | bytes 6148
  82.7 24.9 %copy-start.11 = (f32[512,4]{0,1:T(4,128)S(1)}, f32[512,4]{0,1:T(4,128)}, u32[]{:S(2)}) copy-start(f32[512,4]{0,1:T(4,128)} %param.17) | copy-start | bytes 24580
  83.7 1.3 %copy-start.1 = (f32[1,42,20,512]{3,1,0,2:T(8,128)}, f32[1,42,20,512]{3,1,0,2:T(8,128)S(1)}, u32[]{:S(2)}) copy-start(f32[1,42,20,512]{3,1,0,2:T(8,128)S(1)} %copy_select_fusion) | copy-start | bytes 5160964
  104.2 6.6 %collective-permute-start.4 = (f32[4,2048]{1,0:T(4,128)S(1)}, f32[4,2048]{1,0:T(4,128)S(1)}, u32[]{:S(2)}, u32[]{:S(2)}) collective-permute-start(f32[4,2048]{1,0:T(4,128)S(1)} %all_gather.7), channel_id=1, source_target_pairs={{0,16},{1,17},{2,18},{3,19},{4,20},{5,21},{6,22},{7,23},{8,24},{9,... | collective-permute-start | bytes 98312 | tf_op jit(solution)/shard_map/ppermute | solution.py:25
where the time goes:
time: 122 us
  other arithmetic  52 us (43%)
  waiting for transfers between devices  21.8 us (18%)
  local copies, waits for them, and re-layouts  20.8 us (17%)
  blocking collectives  18.9 us (15%)
  starting transfers between devices  6.99 us (6%)
    concatenate x2, other arithmetic, extended(): x = jnp.concatenate([before, x, after], axis=dim)  25.1 us
    ppermute x2, waiting for transfers between devices, extended(): after = lax.ppermute(first, axis, down)  19.8 us
    all_gather x1, blocking collectives, body(): lax.all_gather(column, 'lev', axis=0, tiled=True)  13.7 us
    neg x2, other arithmetic, advance(): tendency = -(flux_right - flux_left)  9.84 us
    unnamed x32, local copies, waits for them, and re-layouts  5.92 us
    add x2, other arithmetic, advance(): tracer_next = middle[:, 2:] + tendency[:, 2:]  5.57 us
    gather x1, local copies, waits for them, and re-layouts, body(): picked = received[:, sky_point_of_entry]  5.48 us
    all_gather x1, blocking collectives, body(): whole = lax.all_gather(surface, 'tile', axis=1, tiled=True)  5.19 us
  transfers between devices with their start and end apart: 5, of which 4 were waited for; matrix products, arithmetic and copies ran while one was open for 3% of the time, Pallas kernels for 0%

commit v1 on v0

--- a/solution.py
+++ b/solution.py
@@ -1,9 +1,30 @@
+import functools
 import jax
 import jax.numpy as jnp
 from jax import lax
 from jax.sharding import PartitionSpec as P
 
 NFLUX = 4
+
+
+def switch_groups(x0, across):
+    next_value = lax.axis_size(across)
+    parts_out = lax.axis_index(across)
+    b_next, block_next = (next_value, parts_out)
+    g_now, spare = (x0, 1)
+    while spare < b_next:
+        r1 = range(b_next)
+        side_arr = map(lambda j0: (j0, j0 ^ spare), r1)
+        arr_now = list(side_arr)
+        big = lax.ppermute(g_now, axis_name=across, perm=arr_now)
+        piece_out = jnp.concatenate([g_now, big], 0)
+        current_value = jnp.concatenate([big, g_now], 0)
+        g_now = jnp.where(block_next & spare == 0, piece_out, current_value)
+        spare = 2 * spare
+    return g_now
+
+
+advance_tokens_over_axis = functools.partial(switch_groups, across="lev")
 
 
 def extended(x, sides, width):
@@ -72,7 +93,7 @@
     my_rows = lax.dynamic_slice_in_dim(matrix, offset, level_count, 0)
     blended_profiles = jnp.dot(
         my_rows,
-        lax.all_gather(column, "lev", axis=0, tiled=True),
+        advance_tokens_over_axis(column),
         precision=lax.Precision.HIGHEST,
         preferred_element_type=jnp.float32,
     )

time: 122 us -> 119 us (0.975)
  blocking collectives: 18.9 us -> 5.19 us
  waiting for transfers between devices: 21.8 us -> 28.1 us
  starting transfers between devices: 6.99 us -> 11.2 us
    all_gather x1 -> x0, blocking collectives: 13.7 us -> none  [body(): lax.all_gather(column, 'lev', axis=0, tiled=True)]
    ppermute x0 -> x2, starting transfers between devices: none -> 4.23 us  [switch_groups(): big = lax.ppermute(g_now, axis_name=across, perm=arr_now)]
    ppermute x0 -> x2, waiting for transfers between devices: none -> 4.12 us  [switch_groups(): big = lax.ppermute(g_now, axis_name=across, perm=arr_now)]
    slice x1 -> x2, local copies, waits for them, and re-layouts: 3.01 us -> 0.01 us  [body(): joined_quantities[:, 2:].at[0, 0:NFLUX - 1, 0]]
    gather x1, local copies, waits for them, and re-layouts: 5.48 us -> 7.64 us  [body(): picked = received[:, sky_point_of_entry]]
    unnamed x32 -> x30, local copies, waits for them, and re-layouts: 5.92 us -> 7.47 us
    ppermute x1, waiting for transfers between devices: 0.01 us -> 1.39 us  [passed_along(): lax.ppermute(value, axis, [(source, source + steps) for source in range(f...]
    scatter x1, local copies, waits for them, and re-layouts: 1.36 us -> 0.09 us  [body(): joined_quantities[:, 2:].at[0, 0:NFLUX - 1, 0]]
  transfers between devices with their start and end apart: 5 -> 7, of which waited for: 4 -> 7; matrix products, arithmetic and copies ran while one was open for 3% -> 1% of each run, Pallas kernels for 0% -> 0%
where the time goes in v1:
time: 119 us; the launch traced here: 118 us
  other arithmetic  52.5 us (44%)
  waiting for transfers between devices  28.1 us (24%)
  local copies, waits for them, and re-layouts  20.1 us (17%)
  starting transfers between devices  11.2 us (9%)
  blocking collectives  5.19 us (4%)
    concatenate x2, other arithmetic, extended(): x = jnp.concatenate([before, x, after], axis=dim)  25.1 us
    ppermute x2, waiting for transfers between devices, extended(): after = lax.ppermute(first, axis, down)  20.5 us
    neg x2, other arithmetic, advance(): tendency = -(flux_right - flux_left)  9.87 us
    gather x1, local copies, waits for them, and re-layouts, body(): picked = received[:, sky_point_of_entry]  7.64 us
    unnamed x30, local copies, waits for them, and re-layouts  7.47 us
    add x2, other arithmetic, advance(): tracer_next = middle[:, 2:] + tendency[:, 2:]  5.57 us
    all_gather x1, blocking collectives, body(): whole = lax.all_gather(surface, 'tile', axis=1, tiled=True)  5.19 us
    concatenate x3, other arithmetic, advance(): return jnp.concatenate([heat_next[:, None], speed, tracer_next], axis=1)  4.97 us
  transfers between devices with their start and end apart: 7, of which 7 were waited for; matrix products, arithmetic and copies ran while one was open for 1% of the time, Pallas kernels for 0%

profile of v1, /device:TPU:0, one launch (start us, length us, event | category | flops | bytes accessed | tf_op | source)
XLA Modules:
  0.0 118.5 jit_solution(12082512445517099014)
XLA Ops:
  0.7 3.1 %copy.245 = f32[1,40,20,512]{3,0,2,1:T(1,128)S(1)} copy(f32[1,40,20,512]{3,1,2,0:T(8,128)} %param.14) | data formatting | bytes 3276800 | tf_op args[2]
  3.8 2.4 %fusion.8 = f32[1,42,20,512]{3,0,2,1:T(1,128)S(1)} fusion(f32[1,1,20,512]{3,0,2,1:T(1,128)S(1)} %bitcast.86, f32[1,40,20,512]{3,0,2,1:T(1,128)S(1)} %copy.245, f32[1,1,20,512]{3,0,2,1:T(1,128)S(1)} %bitcast.96), kind=kLoop, calls=%fused_computation.17 | loop fusion | flops 860160 | bytes 3440640 | tf_op jit(solution)/shard_map/concatenate | solution.py:79
  6.2 1.2 fusion.45
  7.4 2.5 %collective-permute-start = (f32[1,42,20,1]{3,0,2,1:T(1,128)S(1)}, f32[1,42,20,1]{3,0,2,1:T(1,128)S(1)}, u32[]{:S(2)}, u32[]{:S(2)}) collective-permute-start(f32[1,42,20,1]{3,0,2,1:T(1,128)S(1)} %get-tuple-element.56), channel_id=1, source_target_pairs={{4,0},{8,4},{12,8},{0,12},{5,1},{9,5},{13,9},{1,13},{6,2},{10,6},{... | collective-permute-start | bytes 10088 | tf_op jit(solution)/shard_map/ppermute | solution.py:38
  10.0 10.2 %collective-permute-done = f32[1,42,20,1]{3,0,2,1:T(1,128)S(1)} collective-permute-done((f32[1,42,20,1]{3,0,2,1:T(1,128)S(1)}, f32[1,42,20,1]{3,0,2,1:T(1,128)S(1)}, u32[]{:S(2)}, u32[]{:S(2)}) %collective-permute-start) | collective-permute-done | bytes 3392 | tf_op jit(solution)/shard_map/ppermute | solution.py:38
  20.1 1.1 collective-permute-done.1
  21.2 12.0 %fusion.5 = (f32[1,42,20,513]{3,0,2,1:T(1,128)S(1)}, f32[1,42,20,513]{3,0,2,1:T(1,128)S(1)}) fusion(f32[1,1,20,512]{3,0,2,1:T(1,128)S(1)} %bitcast.87, f32[1,42,20,1]{3,0,2,1:T(1,128)S(1)} %collective-permute-done, f32[1,40,20,512]{3,0,2,1:T(1,128)S(1)} %copy.245, f32[1,1,20,512]{3,0,2,1:T(1,128)S(1)} %bitcast.97, f32[1,42,20,1]{3,0,2,1:T(1,128)S(1)} %collective-permute-done.1), kind=kLoop, calls=%fused_computation.10 | loop fusion | flops 2585520 | bytes 5174400 | tf_op jit(solution)/shard_map/concatenate | solution.py:39
  33.3 4.9 %fusion.17 = f32[1,42,20,512]{3,0,2,1:T(1,128)S(1)} fusion(f32[1,42,20,513]{3,0,2,1:T(1,128)S(1)} %get-tuple-element.55, f32[1,42,20,513]{3,0,2,1:T(1,128)S(1)} %get-tuple-element.54, f32[20,512]{1,0:T(8,128)S(1)} %get-tuple-element.63, f32[20,512]{1,0:T(8,128)S(1)} %get-tuple-element.62, f32[20,512]{1,0:T(8,128)S(1)} %get-tuple-element.64, ...), kind=kLoop, calls=%fused_computation.30 | loop fusion | flops 4300800 | bytes 7045120 | tf_op jit(solution)/shard_map/neg | solution.py:57
  38.3 2.2 %slice_add_fusion.1 = f32[1,40,20,512]{3,0,2,1:T(1,128)S(1)} fusion(f32[1,42,20,512]{3,0,2,1:T(1,128)S(1)} %fusion.17, f32[1,40,20,512]{3,1,2,0:T(8,128)S(1)} %copy-done.2), kind=kLoop, calls=%fused_computation.33 | loop fusion | flops 409600 | bytes 4915200 | tf_op jit(solution)/shard_map/add | solution.py:63
  40.7 2.4 %fusion.9 = f32[1,42,20,512]{3,0,2,1:T(1,128)S(1)} fusion(f32[1,1,20,512]{3,0,2,1:T(1,128)S(1)} %bitcast.89, f32[1,40,20,512]{3,0,2,1:T(1,128)S(1)} %slice_add_fusion.1, f32[1,1,20,512]{3,0,2,1:T(1,128)S(1)} %bitcast.93), kind=kLoop, calls=%fused_computation.18 | loop fusion | flops 860160 | bytes 3440640 | tf_op jit(solution)/shard_map/concatenate | solution.py:64
  43.1 2.1 %fusion.44 = (f32[1,42,20,1]{3,0,2,1:T(1,128)}, f32[1,42,20,1]{3,0,2,1:T(1,128)}) fusion(f32[1,42,20,512]{3,0,2,1:T(1,128)S(1)} %fusion.9), kind=kLoop, calls=%fused_computation.87 | loop fusion | bytes 13440 | tf_op jit(solution)/shard_map/slice | solution.py:36
  45.2 1.1 collective-permute-start.2
  46.3 10.4 %collective-permute-done.2 = f32[1,42,20,1]{3,0,2,1:T(1,128)} collective-permute-done((f32[1,42,20,1]{3,0,2,1:T(1,128)}, f32[1,42,20,1]{3,0,2,1:T(1,128)}, u32[]{:S(2)}, u32[]{:S(2)}) %collective-permute-start.2) | collective-permute-done | bytes 3392 | tf_op jit(solution)/shard_map/ppermute | solution.py:38
  56.7 1.0 collective-permute-done.3
  57.7 13.0 %fusion.7 = (f32[1,42,20,513]{3,0,2,1:T(1,128)S(1)}, f32[1,42,20,513]{3,0,2,1:T(1,128)S(1)}) fusion(f32[1,1,20,512]{3,0,2,1:T(1,128)S(1)} %bitcast.90, f32[1,42,20,1]{3,0,2,1:T(1,128)} %collective-permute-done.2, f32[1,40,20,512]{3,0,2,1:T(1,128)S(1)} %slice_add_fusion.1, f32[1,1,20,512]{3,0,2,1:T(1,128)S(1)} %bitcast.94, ...), kind=kLoop, calls=%fused_computation.12 | loop fusion | flops 2585520 | bytes 5174400 | tf_op jit(solution)/shard_map/concatenate | solution.py:39
  70.8 4.9 %fusion.18 = f32[1,42,20,512]{3,0,2,1:T(1,128)S(1)} fusion(f32[1,42,20,513]{3,0,2,1:T(1,128)S(1)} %get-tuple-element.51, f32[1,42,20,513]{3,0,2,1:T(1,128)S(1)} %get-tuple-element.50, f32[20,512]{1,0:T(8,128)S(1)} %get-tuple-element.59, f32[20,512]{1,0:T(8,128)S(1)} %get-tuple-element.58, f32[20,512]{1,0:T(8,128)S(1)} %get-tuple-element.64, ...), kind=kLoop, calls=%fused_computation.31 | loop fusion | flops 4300800 | bytes 7045120 | tf_op jit(solution)/shard_map/neg | solution.py:57
  75.9 3.3 %slice_add_fusion = f32[1,40,20,512]{3,0,2,1:T(1,128)S(1)} fusion(f32[1,40,20,512]{3,0,2,1:T(1,128)S(1)} %slice_add_fusion.1, f32[1,42,20,512]{3,0,2,1:T(1,128)S(1)} %fusion.18), kind=kLoop, calls=%fused_computation.32 | loop fusion | flops 409600 | bytes 4915200 | tf_op jit(solution)/shard_map/add | solution.py:63
  79.3 2.4 %fusion.10 = f32[1,42,20,512]{3,0,2,1:T(1,128)S(1)} fusion(f32[1,1,20,512]{3,0,2,1:T(1,128)S(1)} %bitcast.92, f32[1,40,20,512]{3,0,2,1:T(1,128)S(1)} %slice_add_fusion, f32[1,1,20,512]{3,0,2,1:T(1,128)S(1)} %add_bitcast_fusion), kind=kLoop, calls=%fused_computation.19 | loop fusion | flops 860160 | bytes 3440640 | tf_op jit(solution)/shard_map/concatenate | solution.py:64
  81.7 0.5 copy_select_fusion
  82.2 1.3 %copy-done.1 = f32[1,42,20,512]{3,2,1,0:T(8,128)} copy-done((f32[1,42,20,512]{3,2,1,0:T(8,128)}, f32[1,42,20,512]{3,2,1,0:T(8,128)S(1)}, u32[]{:S(2)}) %copy-start.1) | copy-done | bytes 1720344
  83.5 1.6 %collective-permute-start.4 = (f32[20,512]{1,0:T(8,128)S(1)}, f32[20,512]{1,0:T(8,128)S(1)}, u32[]{:S(2)}, u32[]{:S(2)}) collective-permute-start(f32[20,512]{1,0:T(8,128)S(1)} %slice_bitcast_fusion), channel_id=1, source_target_pairs={{0,1},{1,0},{2,3},{3,2},{4,5},{5,4},{6,7},{7,6},{8,9},{9,8},{10,11... | collective-permute-start | bytes 122888 | tf_op jit(solution)/shard_map/ppermute | solution.py:19
  85.5 2.2 %collective-permute-done.4 = f32[20,512]{1,0:T(8,128)S(1)} collective-permute-done((f32[20,512]{1,0:T(8,128)S(1)}, f32[20,512]{1,0:T(8,128)S(1)}, u32[]{:S(2)}, u32[]{:S(2)}) %collective-permute-start.4) | collective-permute-done | bytes 40992 | tf_op jit(solution)/shard_map/ppermute | solution.py:19
  87.7 2.7 %collective-permute-start.5 = (f32[40,512]{1,0:T(8,128)S(1)}, f32[40,512]{1,0:T(8,128)S(1)}, u32[]{:S(2)}, u32[]{:S(2)}) collective-permute-start(f32[40,512]{1,0:T(8,128)S(1)} %maximum_select_fusion.2), channel_id=1, source_target_pairs={{0,2},{1,3},{2,0},{3,1},{4,6},{5,7},{6,4},{7,5},{8,10},{9,11},{10,... | collective-permute-start | bytes 245768 | tf_op jit(solution)/shard_map/ppermute | solution.py:19
  90.3 0.8 slice.173
  91.1 1.9 %collective-permute-done.5 = f32[40,512]{1,0:T(8,128)S(1)} collective-permute-done((f32[40,512]{1,0:T(8,128)S(1)}, f32[40,512]{1,0:T(8,128)S(1)}, u32[]{:S(2)}, u32[]{:S(2)}) %collective-permute-start.5) | collective-permute-done | bytes 81952 | tf_op jit(solution)/shard_map/ppermute | solution.py:19
  93.3 5.2 %all_gather.3 = f32[4,2048]{1,0:T(4,128)S(1)} all-gather(f32[4,512]{1,0:T(4,128)S(1)} %pad_maximum_fusion.7), channel_id=1, replica_groups=mesh['comp'=2,'tile'=4,'lev'=4] {'tile'}, dimensions={1}, use_global_device_ids=true | all-gather | bytes 40960 | tf_op jit(solution)/shard_map/all_gather | solution.py:103
  98.5 3.4 %collective-permute-start.6 = (f32[4,2048]{1,0:T(4,128)S(1)}, f32[4,2048]{1,0:T(4,128)S(1)}, u32[]{:S(2)}, u32[]{:S(2)}) collective-permute-start(f32[4,2048]{1,0:T(4,128)S(1)} %all_gather.3), channel_id=1, source_target_pairs={{0,16},{1,17},{2,18},{3,19},{4,20},{5,21},{6,22},{7,23},{8,24},{9,... | collective-permute-start | bytes 98312 | tf_op jit(solution)/shard_map/ppermute | solution.py:46
  102.1 1.4 %collective-permute-done.6 = f32[4,2048]{1,0:T(4,128)S(1)} collective-permute-done((f32[4,2048]{1,0:T(4,128)S(1)}, f32[4,2048]{1,0:T(4,128)S(1)}, u32[]{:S(2)}, u32[]{:S(2)}) %collective-permute-start.6) | collective-permute-done | bytes 32800 | tf_op jit(solution)/shard_map/ppermute | solution.py:46
  103.9 7.6 %gather_fusion = f32[2048,4]{1,0:T(8,128)} fusion(f32[4,2048]{0,1:T(8,128)S(1)} %copy.252, s32[2048]{0:T(1024)S(1)} %broadcast_clamp_fusion), kind=kCustom, calls=%fused_computation | custom fusion | bytes 73728 | tf_op jit(solution)/shard_map/gather | solution.py:105
  111.5 3.8 %multiply_reduce_fusion = f32[512,4]{1,0:T(8,128)S(1)} fusion(f32[512,4,4]{2,1,0:T(4,128)} %bitcast.85, f32[512,4]{1,0:T(8,128)S(1)} %copy.253), kind=kLoop, calls=%fused_computation.34 | loop fusion | flops 14336 | bytes 49152 | tf_op jit(solution)/shard_map/reduce_sum | solution.py:106
  115.6 2.1 %copy.257 = f32[1,40,20,512]{3,1,2,0:T(8,128)} copy(f32[1,40,20,512]{3,2,1,0:T(8,128)S(1)} %scatter.9) | data formatting | bytes 3276800
  117.8 0.7 copy.256
  (55 shorter events, 1.9 us)
Async XLA Ops:
  0.6 92.4 %copy-start = (f32[1,80,80]{2,1,0:T(8,128)S(1)}, f32[1,80,80]{2,1,0:T(8,128)}, u32[]{:S(2)}) copy-start(f32[1,80,80]{2,1,0:T(8,128)} %param.16) | copy-start | bytes 76804
  0.6 3.2 %copy-start.3 = (f32[1,20,512]{2,0,1:T(1,128)S(1)}, f32[1,20,512]{2,0,1:T(1,128)}, u32[]{:S(2)}) copy-start(f32[1,20,512]{2,0,1:T(1,128)} %param.13) | copy-start | bytes 122884
  0.7 3.2 %copy-start.4 = (f32[1,20,512]{2,0,1:T(1,128)S(1)}, f32[1,20,512]{2,0,1:T(1,128)}, u32[]{:S(2)}) copy-start(f32[1,20,512]{2,0,1:T(1,128)} %param.12) | copy-start | bytes 122884
  7.4 12.7 %collective-permute-start = (f32[1,42,20,1]{3,0,2,1:T(1,128)S(1)}, f32[1,42,20,1]{3,0,2,1:T(1,128)S(1)}, u32[]{:S(2)}, u32[]{:S(2)}) collective-permute-start(f32[1,42,20,1]{3,0,2,1:T(1,128)S(1)} %get-tuple-element.56), channel_id=1, source_target_pairs={{4,0},{8,4},{12,8},{0,12},{5,1},{9,5},{13,9},{1,13},{6,2},{10,6},{... | collective-permute-start | bytes 10088 | tf_op jit(solution)/shard_map/ppermute | solution.py:38
  9.9 11.3 %collective-permute-start.1 = (f32[1,42,20,1]{3,0,2,1:T(1,128)S(1)}, f32[1,42,20,1]{3,0,2,1:T(1,128)S(1)}, u32[]{:S(2)}, u32[]{:S(2)}) collective-permute-start(f32[1,42,20,1]{3,0,2,1:T(1,128)S(1)} %get-tuple-element.57), channel_id=1, source_target_pairs={{0,4},{4,8},{8,12},{12,0},{1,5},{5,9},{9,13},{13,1},{2,6},{6,10},{... | collective-permute-start | bytes 10088 | tf_op jit(solution)/shard_map/ppermute | solution.py:37
  9.9 23.3 %copy-start.5 = (f32[20,512]{1,0:T(8,128)}, f32[20,512]{1,0:T(8,128)S(1)}, u32[]{:S(2)}) copy-start(f32[20,512]{1,0:T(8,128)S(1)} %get-tuple-element.65) | copy-start | bytes 122884
  33.3 5.0 %copy-start.2 = (f32[1,40,20,512]{3,1,2,0:T(8,128)S(1)}, f32[1,40,20,512]{3,1,2,0:T(8,128)}, u32[]{:S(2)}) copy-start(f32[1,40,20,512]{3,1,2,0:T(8,128)} %param.14) | copy-start | bytes 4915204
  38.3 2.3 %copy-start.7 = (f32[1,20,512]{2,0,1:T(1,128)S(1)}, f32[1,20,512]{2,0,1:T(1,128)}, u32[]{:S(2)}) copy-start(f32[1,20,512]{2,0,1:T(1,128)} %param.15) | copy-start | bytes 122884
  45.2 11.5 %collective-permute-start.2 = (f32[1,42,20,1]{3,0,2,1:T(1,128)}, f32[1,42,20,1]{3,0,2,1:T(1,128)}, u32[]{:S(2)}, u32[]{:S(2)}) collective-permute-start(f32[1,42,20,1]{3,0,2,1:T(1,128)} %get-tuple-element.52), channel_id=1, source_target_pairs={{4,0},{8,4},{12,8},{0,12},{5,1},{9,5},{13,9},{1,13},{6,2},{10,6},{... | collective-permute-start | bytes 10088 | tf_op jit(solution)/shard_map/ppermute | solution.py:38
  46.3 11.4 %collective-permute-start.3 = (f32[1,42,20,1]{3,0,2,1:T(1,128)}, f32[1,42,20,1]{3,0,2,1:T(1,128)}, u32[]{:S(2)}, u32[]{:S(2)}) collective-permute-start(f32[1,42,20,1]{3,0,2,1:T(1,128)} %get-tuple-element.53), channel_id=1, source_target_pairs={{0,4},{4,8},{8,12},{12,0},{1,5},{5,9},{9,13},{13,1},{2,6},{6,10},{... | collective-permute-start | bytes 10088 | tf_op jit(solution)/shard_map/ppermute | solution.py:37
  46.3 24.5 %copy-start.6 = (f32[20,512]{1,0:T(8,128)S(1)}, f32[20,512]{1,0:T(8,128)}, u32[]{:S(2)}) copy-start(f32[20,512]{1,0:T(8,128)} %copy-done.5) | copy-start | bytes 122884
  70.8 4.9 %copy-start.8 = (f32[1,20,512]{2,0,1:T(1,128)S(1)}, f32[1,20,512]{2,0,1:T(1,128)}, u32[]{:S(2)}) copy-start(f32[1,20,512]{2,0,1:T(1,128)} %param.15) | copy-start | bytes 122884
  81.7 3.5 %copy-start.10 = (s32[512,4]{0,1:T(4,128)S(1)}, s32[512,4]{0,1:T(4,128)}, u32[]{:S(2)}) copy-start(s32[512,4]{0,1:T(4,128)} %param.18) | copy-start | bytes 24580
  81.7 20.2 %copy-start.11 = (s32[512]{0:T(512)S(1)}, s32[512]{0:T(512)}, u32[]{:S(2)}) copy-start(s32[512]{0:T(512)} %param.19) | copy-start | bytes 6148
  81.7 20.3 %copy-start.9 = (f32[512,4]{0,1:T(4,128)S(1)}, f32[512,4]{0,1:T(4,128)}, u32[]{:S(2)}) copy-start(f32[512,4]{0,1:T(4,128)} %param.17) | copy-start | bytes 24580
  82.2 1.3 %copy-start.1 = (f32[1,42,20,512]{3,2,1,0:T(8,128)}, f32[1,42,20,512]{3,2,1,0:T(8,128)S(1)}, u32[]{:S(2)}) copy-start(f32[1,42,20,512]{3,2,1,0:T(8,128)S(1)} %copy_select_fusion) | copy-start | bytes 5160964
  83.5 4.1 %collective-permute-start.4 = (f32[20,512]{1,0:T(8,128)S(1)}, f32[20,512]{1,0:T(8,128)S(1)}, u32[]{:S(2)}, u32[]{:S(2)}) collective-permute-start(f32[20,512]{1,0:T(8,128)S(1)} %slice_bitcast_fusion), channel_id=1, source_target_pairs={{0,1},{1,0},{2,3},{3,2},{4,5},{5,4},{6,7},{7,6},{8,9},{9,8},{10,11... | collective-permute-start | bytes 122888 | tf_op jit(solution)/shard_map/ppermute | solution.py:19
  87.7 5.4 %collective-permute-start.5 = (f32[40,512]{1,0:T(8,128)S(1)}, f32[40,512]{1,0:T(8,128)S(1)}, u32[]{:S(2)}, u32[]{:S(2)}) collective-permute-start(f32[40,512]{1,0:T(8,128)S(1)} %maximum_select_fusion.2), channel_id=1, source_target_pairs={{0,2},{1,3},{2,0},{3,1},{4,6},{5,7},{6,4},{7,5},{8,10},{9,11},{10,... | collective-permute-start | bytes 245768 | tf_op jit(solution)/shard_map/ppermute | solution.py:19
  98.5 5.0 %collective-permute-start.6 = (f32[4,2048]{1,0:T(4,128)S(1)}, f32[4,2048]{1,0:T(4,128)S(1)}, u32[]{:S(2)}, u32[]{:S(2)}) collective-permute-start(f32[4,2048]{1,0:T(4,128)S(1)} %all_gather.3), channel_id=1, source_target_pairs={{0,16},{1,17},{2,18},{3,19},{4,20},{5,21},{6,22},{7,23},{8,24},{9,... | collective-permute-start | bytes 98312 | tf_op jit(solution)/shard_map/ppermute | solution.py:46
  103.9 11.7 %slice-start = ((f32[1,42,20,512]{3,2,1,0:T(8,128)}), f32[1,40,20,512]{3,2,1,0:T(8,128)S(1)}, s32[]{:S(2)}) async-start(f32[1,42,20,512]{3,2,1,0:T(8,128)} %copy-done.1), calls=%async_computation | async-start | bytes 3932160 | tf_op jit(solution)/shard_map/slice | solution.py:114
